TPU v7x, 512 devices: a whole 4x4x16 slice. The times are simulated.
512 devices in a mesh: tok: 16 (over y, x), hid: 32 (over z, core).
Axes of the slice: x: 4, y: 4, z: 16, core: 2. Of those that a mesh axis runs over, the one named last changes fastest.
Arguments:
- tokens: bfloat16 [2048, 8192], P('tok', 'hid'), may hold values from -6 to 6
- gate_weight: bfloat16 [8192, 16384], P('tok', 'hid'), may hold values from -0.09375 to 0.09375
- up_weight: bfloat16 [8192, 16384], P('tok', 'hid'), may hold values from -0.09375 to 0.09375
- down_weight: bfloat16 [16384, 8192], P('hid', 'tok'), may hold values from -0.0625 to 0.0625
- gate_keep: int32 [64, 128], P('tok', 'hid'), may hold values from 0 to 1, as said below
- up_keep: int32 [64, 128], P('tok', 'hid'), may hold values from 0 to 1, as said below
- down_keep: int32 [128, 64], P('hid', 'tok'), may hold values from 0 to 1, as said below
Outputs:
- mixed: bfloat16 [2048, 8192], P('hid', 'tok')
Inputs may be any that keep to these rules, and one draw needn't show every extreme that they name: `gate_keep`: in every device's shard of 4 x 4 blocks of a mask, between 4 and 8 blocks are kept; in every mask some shard keeps exactly 8. Shards of down_keep are 4 x 4. `up_keep`: as for gate_keep, drawn independently. `down_keep`: as for gate_keep, drawn independently.
All inputs are finite; a program needn't handle non-finite values.
Results may differ from a plain program's by a relative error of at most 0.0049.
Values may be sent and summed in bfloat16 or wider, within the bound.
A program may use at most 64 MiB of HBM per device.

v0:
```python
import jax
import jax.numpy as jnp
from jax import lax
from jax.sharding import PartitionSpec as P


def pack_blocks(weight, keep_mask):
    block_rows, block_cols = keep_mask.shape
    side = weight.shape[0] // block_rows
    capacity = block_rows * block_cols // 2
    flat_keep = keep_mask.reshape(-1)
    block_rank = jnp.cumsum(flat_keep) - 1
    slot_ids = jnp.arange(capacity, dtype=jnp.int32)
    select = ((block_rank[None, :] == slot_ids[:, None]) & (flat_keep[None, :] == 1)).astype(
        weight.dtype
    )
    blocks = weight.reshape(block_rows, side, block_cols, side).transpose(0, 2, 1, 3)
    blocks = blocks.reshape(block_rows * block_cols, side, side)
    packed = jnp.einsum("sb,bij->sij", select, blocks, preferred_element_type=jnp.float32)
    return (packed.astype(weight.dtype)[None], flat_keep[None])


def unpack_blocks(packed, flags, block_rows, block_cols):
    shards, capacity, side, _ = packed.shape
    block_rank = jnp.cumsum(flags, axis=1) - 1
    slot_ids = jnp.arange(capacity, dtype=jnp.int32)
    select = (
        (block_rank[:, :, None] == slot_ids[None, None, :]) & (flags[:, :, None] == 1)
    ).astype(packed.dtype)
    dense_tiles = jnp.einsum(
        "kbs,ksij->kbij", select, packed, preferred_element_type=jnp.float32
    ).astype(packed.dtype)
    dense_tiles = dense_tiles.reshape(shards, block_rows, block_cols, side, side).transpose(
        0, 1, 3, 2, 4
    )
    return dense_tiles.reshape(shards * block_rows * side, block_cols * side)


def prune_local(weight, keep_mask):
    block_rows, block_cols = keep_mask.shape
    row_count, col_count = weight.shape
    tiles = weight.reshape(block_rows, row_count // block_rows, block_cols, col_count // block_cols)
    kept = tiles * keep_mask[:, None, :, None].astype(weight.dtype)
    return kept.reshape(row_count, col_count)


def local(tokens, gate_weight, up_weight, down_weight, gate_keep, up_keep, down_keep):
    features_all = lax.all_gather(tokens, "hid", axis=1, tiled=True)
    block_rows, block_cols = gate_keep.shape
    gate_packed, gate_flags = pack_blocks(gate_weight, gate_keep)
    up_packed, up_flags = pack_blocks(up_weight, up_keep)

    def add_product(packed, flags):
        dense_strip = unpack_blocks(packed, flags, block_rows, block_cols)
        return jnp.dot(features_all, dense_strip, preferred_element_type=jnp.float32)

    def add_single(arrived):
        return add_product(arrived[0], arrived[1])

    gate_out = add_single(
        (
            lax.all_gather(gate_packed, "tok", axis=0, tiled=True),
            lax.all_gather(gate_flags, "tok", axis=0, tiled=True),
        )
    )
    up_out = add_single(
        (
            lax.all_gather(up_packed, "tok", axis=0, tiled=True),
            lax.all_gather(up_flags, "tok", axis=0, tiled=True),
        )
    )
    hidden = (jax.nn.silu(gate_out) * up_out).astype(jnp.bfloat16)
    down_dense = prune_local(down_weight, down_keep)
    partial_sums = jnp.dot(
        lax.all_gather(hidden, "tok", axis=0, tiled=True),
        down_dense,
        preferred_element_type=jnp.float32,
    )
    mixed = lax.psum_scatter(partial_sums, "hid", scatter_dimension=0, tiled=True)
    return mixed.astype(jnp.bfloat16)


def solution(mesh):
    return jax.shard_map(
        local,
        mesh=mesh,
        in_specs=(
            P("tok", "hid"),
            P("tok", "hid"),
            P("tok", "hid"),
            P("hid", "tok"),
            P("tok", "hid"),
            P("tok", "hid"),
            P("hid", "tok"),
        ),
        out_specs=P("hid", "tok"),
        check_vma=False,
    )
```

profile of v0, /device:TPU:2, one launch (start us, length us, event | category | flops | bytes accessed | tf_op | source)
XLA Modules:
  0.0 433.2 jit_solution(12943204567747657550)
XLA Ops:
  6.5 0.8 reshape.145
  7.4 0.7 broadcast_compare_fusion.3
  8.1 1.2 reshape.124
  9.2 0.2 copy.25
  9.4 0.1 add_reduce_fusion.1
  9.6 0.1 eq.90
  9.7 0.9 convolution_convert_fusion.3
  10.7 1.2 reshape.129
  11.8 0.2 copy.29
  12.2 0.1 eq.99
  12.3 0.1 add_reduce_fusion
  12.4 0.9 convolution_convert_fusion.2
  13.4 0.7 all-gather.9.cloned.1.call-update
  14.3 23.2 %all-gather.2 = s32[16,1,16]{2,1,0:T(1,128)S(1)} all-gather(s32[1,1,16]{2,1,0:T(1,128)S(1)} %reshape.135), channel_id=1, replica_groups=mesh['tok'=16,'hid'=32] {'tok'}, dimensions={0}, use_global_device_ids=true | all-gather | bytes 1088 | tf_op jit(solution)/shard_map/all_gather | solution.py:63
  37.4 0.2 reduce_window_sum.26
  37.6 18.3 %all-gather.3 = s32[16,1,16]{2,1,0:T(1,128)S(1)} all-gather(s32[1,1,16]{2,1,0:T(1,128)S(1)} %reshape.137), channel_id=1, replica_groups=mesh['tok'=16,'hid'=32] {'tok'}, dimensions={0}, use_global_device_ids=true | all-gather | bytes 1088 | tf_op jit(solution)/shard_map/all_gather | solution.py:69
  55.9 0.2 reduce_window_sum.27
  56.1 31.0 %all-gather.13.cloned.1.call-done = bf16[128,128,128]{2,0,1:T(8,128)(2,1)} async-done(((bf16[8,128,128]{2,0,1:T(8,128)(2,1)}), bf16[128,128,128]{2,0,1:T(8,128)(2,1)}) %all-gather.13.cloned.1.call-update) | async-done | bytes 4194320 | tf_op jit(solution)/shard_map/all_gather | solution.py:62
  87.1 4.2 convolution_convert_fusion.1
  91.3 5.9 %copy.27 = bf16[16,4,4,128,128]{4,2,3,1,0:T(4,128)(2,1)} copy(bf16[16,4,4,128,128]{4,2,1,3,0:T(4,128)(2,1)S(1)} %bitcast.70) | data formatting | bytes 16777216 | tf_op jit(solution)/shard_map/reshape | solution.py:33
  97.2 64.5 %all-gather.15.cloned.1.call-done = bf16[128,128,128]{2,0,1:T(8,128)(2,1)} async-done(((bf16[8,128,128]{2,0,1:T(8,128)(2,1)}), bf16[128,128,128]{2,0,1:T(8,128)(2,1)}) %all-gather.15.cloned.1.call-update) | async-done | bytes 4194320 | tf_op jit(solution)/shard_map/all_gather | solution.py:68
  161.7 4.2 convolution_convert_fusion
  165.9 5.9 %copy.31 = bf16[16,4,4,128,128]{4,2,3,1,0:T(4,128)(2,1)} copy(bf16[16,4,4,128,128]{4,2,1,3,0:T(4,128)(2,1)S(1)} %bitcast.71) | data formatting | bytes 16777216 | tf_op jit(solution)/shard_map/reshape | solution.py:33
  171.8 64.5 %all-gather.9.cloned.1.call-done = bf16[128,8192]{1,0:T(8,128)(2,1)} async-done(((bf16[128,256]{1,0:T(8,128)(2,1)}), bf16[128,8192]{1,0:T(8,128)(2,1)}) %all-gather.9.cloned.1.call-update) | async-done | bytes 2097168 | tf_op jit(solution)/shard_map/all_gather | solution.py:48
  236.4 6.5 %fusion.8 = f32[128,512]{0,1:T(8,128)S(1)} fusion(bf16[128,8192]{1,0:T(8,128)(2,1)} %all-gather.9.cloned.1.call-done, bf16[1024,8,4,128]{3,2,1,0:T(4,128)(2,1)} %bitcast.72), kind=kOutput, calls=%fused_computation.12 | convolution fusion | flops 1073741824 | bytes 10747904 | tf_op jit(solution)/shard_map/dot_general | solution.py:55
  242.8 0.5 copy-done.5
  243.3 3.3 fusion.17
  246.7 58.0 %all-gather.11.cloned.1.call-done = bf16[2048,512]{0,1:T(8,128)(2,1)} async-done(((bf16[128,512]{0,1:T(8,128)(2,1)}), bf16[2048,512]{0,1:T(8,128)(2,1)}) %all-gather.11.cloned.1.call-update) | async-done | bytes 2097168 | tf_op jit(solution)/shard_map/all_gather | solution.py:75
  304.6 0.2 mul.20
  304.8 4.8 %fusion.20 = f32[2048,512]{1,0:T(8,128)} fusion(bf16[2048,512]{0,1:T(8,128)(2,1)} %all-gather.11.cloned.1.call-done, bf16[512,512]{1,0:T(8,128)(2,1)S(1)} %copy-done.1, bf16[64,8,4,128]{3,2,1,0:T(4,128)(2,1)S(1)} %bitcast.74), kind=kOutput, calls=%fused_computation.17 | convolution fusion | flops 1074003968 | bytes 7340032 | tf_op jit(solution)/shard_map/dot_general | solution.py:74
  309.7 115.4 %reduce-scatter.2.cloned.1.call-done = f32[64,512]{1,0:T(8,128)} async-done(((f32[2048,512]{1,0:T(8,128)}), f32[64,512]{1,0:T(8,128)}) %reduce-scatter.2.cloned.1.call-update) | async-done | bytes 131088 | tf_op jit(solution)/shard_map/reduce_scatter | solution.py:79
  425.1 1.5 convert_element_type.32
  (31 shorter events, 0.6 us)
Async XLA Ops:
  6.5 7.6 %copy-start.2 = (s32[4,4]{1,0:T(4,128)S(1)}, s32[4,4]{1,0:T(4,128)}, u32[]{:S(2)}) copy-start(s32[4,4]{1,0:T(4,128)} %param.11) | copy-start | bytes 196
  6.5 5.5 %copy-start.3 = (s32[4,4]{1,0:T(4,128)S(1)}, s32[4,4]{1,0:T(4,128)}, u32[]{:S(2)}) copy-start(s32[4,4]{1,0:T(4,128)} %param.12) | copy-start | bytes 196
  6.5 80.5 %all-gather.13.cloned.1.call-start = ((), (), s32[]{:S(2)}) async-start(), calls=%async_computation.4 | async-start | bytes 4456448 | tf_op jit(solution)/shard_map/all_gather | solution.py:62
  10.6 151.0 %all-gather.15.cloned.1.call-start = ((), (), s32[]{:S(2)}) async-start(), calls=%async_computation.5 | async-start | bytes 4456448 | tf_op jit(solution)/shard_map/all_gather | solution.py:68
  13.3 223.0 %all-gather.9.cloned.1.call-start = ((), (), s32[]{:S(2)}) async-start(), calls=%async_computation.1 | async-start | bytes 2162688 | tf_op jit(solution)/shard_map/all_gather | solution.py:48
  14.1 290.6 %all-gather.11.cloned.1.call-start = ((), (), s32[]{:S(2)}) async-start(), calls=%async_computation.2 | async-start | bytes 2228224 | tf_op jit(solution)/shard_map/all_gather | solution.py:75
  236.4 6.5 %copy-start = (bf16[16,4,4,128,128]{4,2,3,1,0:T(4,128)(2,1)S(1)}, bf16[16,4,4,128,128]{4,2,3,1,0:T(4,128)(2,1)}, u32[]{:S(2)}) copy-start(bf16[16,4,4,128,128]{4,2,3,1,0:T(4,128)(2,1)} %copy.31) | copy-start | bytes 25165828
  236.4 7.0 %copy-start.5 = (bf16[128,8192]{1,0:T(8,128)(2,1)S(1)}, bf16[128,8192]{1,0:T(8,128)(2,1)}, u32[]{:S(2)}) copy-start(bf16[128,8192]{1,0:T(8,128)(2,1)} %all-gather.9.cloned.1.call-done) | copy-start | bytes 6291460
  243.3 3.3 copy-start.4
  243.3 61.5 %copy-start.1 = (bf16[512,512]{1,0:T(8,128)(2,1)S(1)}, bf16[512,512]{1,0:T(8,128)(2,1)}, u32[]{:S(2)}) copy-start(bf16[512,512]{1,0:T(8,128)(2,1)} %param.10) | copy-start | bytes 1572868
  246.6 178.5 %reduce-scatter.2.cloned.1.call-start = ((), (), s32[]{:S(2)}) async-start(), calls=%async_computation.3 | async-start | bytes 4325376 | tf_op jit(solution)/shard_map/reduce_scatter | solution.py:79
Sparse Core Ops, SparseCore 0:
  10.7 76.2 all-gather.12
  90.0 71.5 all-gather.14
  163.7 72.5 all-gather.8
  246.7 57.8 all-gather.10
  309.8 115.2 reduce-scatter.1
where the time goes:
time: 434 us; the launch traced here: 433 us
  waiting for transfers between devices  334 us (77%)
  blocking collectives  41.4 us (10%)
  matrix products  24.9 us (6%)
  local copies, waits for them, and re-layouts  16.4 us (4%)
  between operations  13.3 us (3%)
    reduce_scatter x1, waiting for transfers between devices, local(): lax.psum_scatter(partial_sums, 'hid', scatter_dimension=0, tiled=True)  115 us
    all_gather x1, waiting for transfers between devices, local(): features_all = lax.all_gather(tokens, 'hid', axis=1, tiled=True)  64.5 us
    all_gather x1, waiting for transfers between devices, local(): lax.all_gather(up_packed, 'tok', axis=0, tiled=True)  64.5 us
    all_gather x1, waiting for transfers between devices, local(): lax.all_gather(hidden, 'tok', axis=0, tiled=True)  58 us
    all_gather x1, waiting for transfers between devices, local(): lax.all_gather(gate_packed, 'tok', axis=0, tiled=True)  31 us
    all_gather x1, blocking collectives, local(): lax.all_gather(gate_flags, 'tok', axis=0, tiled=True)  23.2 us
    all_gather x1, blocking collectives, local(): lax.all_gather(up_flags, 'tok', axis=0, tiled=True)  18.3 us
    reshape x2, local copies, waits for them, and re-layouts, unpack_blocks(): dense_tiles.reshape(shards, block_rows, block_cols, side, side)  11.8 us
  transfers between devices with their start and end apart: 5, of which 5 were waited for; matrix products, arithmetic and copies ran while one was open for 5% of the time, Pallas kernels for 0%

commit v1 on v0

--- a/solution.py
+++ b/solution.py
@@ -1,7 +1,18 @@
+import functools
 import jax
 import jax.numpy as jnp
 from jax import lax
 from jax.sharding import PartitionSpec as P
+
+
+def form_heaps(array_here, dim_k):
+    outer = jax.lax.psum(1, "tok")
+    y_new = jnp.stack([array_here] * outer)
+    taken_in = jax.lax.all_to_all(y_new, "tok", 0, 0)
+    return jnp.concatenate(taken_in, axis=dim_k)
+
+
+match_strings = functools.partial(form_heaps, dim_k=0)
 
 
 def pack_blocks(weight, keep_mask):
@@ -64,10 +75,7 @@
         )
     )
     up_out = add_single(
-        (
-            lax.all_gather(up_packed, "tok", axis=0, tiled=True),
-            lax.all_gather(up_flags, "tok", axis=0, tiled=True),
-        )
+        (match_strings(up_packed), lax.all_gather(up_flags, "tok", axis=0, tiled=True))
     )
     hidden = (jax.nn.silu(gate_out) * up_out).astype(jnp.bfloat16)
     down_dense = prune_local(down_weight, down_keep)

time: 434 us -> 397 us (0.915)
  the two profiles are of different devices: /device:TPU:2 before, /device:TPU:14 now
where the time goes in v1:
time: 397 us; the launch traced here: 396 us
  waiting for transfers between devices  242 us (61%)
  blocking collectives  84.9 us (21%)
  matrix products  24.1 us (6%)
  local copies, waits for them, and re-layouts  19.1 us (5%)
  between operations  13.3 us (3%)
  starting transfers between devices  10.3 us (3%)
    reduce_scatter x1, waiting for transfers between devices, local(): lax.psum_scatter(partial_sums, 'hid', scatter_dimension=0, tiled=True)  117 us
    all_gather x1, waiting for transfers between devices, local(): features_all = lax.all_gather(tokens, 'hid', axis=1, tiled=True)  65.8 us
    all_gather x1, blocking collectives, local(): lax.all_gather(gate_flags, 'tok', axis=0, tiled=True)  65.5 us
    all_gather x1, waiting for transfers between devices, local(): lax.all_gather(hidden, 'tok', axis=0, tiled=True)  56.7 us
    all_gather x1, blocking collectives, local(): lax.all_gather(up_flags, 'tok', axis=0, tiled=True)  19.4 us
    reshape x2, local copies, waits for them, and re-layouts, unpack_blocks(): dense_tiles.reshape(shards, block_rows, block_cols, side, side)  11.8 us
    all_to_all x1, starting transfers between devices, form_heaps(): taken_in = jax.lax.all_to_all(y_new, 'tok', 0, 0)  10.1 us
    dot_general x2, matrix products, add_product(): jnp.dot(features_all, dense_strip, preferred_element_type=jnp.float32)  9.72 us
  transfers between devices with their start and end apart: 5, of which 4 were waited for; matrix products, arithmetic and copies ran while one was open for 6% of the time, Pallas kernels for 0%

profile of v1, /device:TPU:14, one launch (start us, length us, event | category | flops | bytes accessed | tf_op | source)
XLA Modules:
  0.0 396.5 jit_solution(8444089440708936000)
XLA Ops:
  6.5 0.8 reshape.150
  7.3 0.7 broadcast_compare_fusion.3
  8.0 1.2 reshape.129
  9.2 0.2 copy.23
  9.4 0.1 add_reduce_fusion.1
  9.6 0.9 convolution_convert_fusion.3
  10.5 1.2 reshape.134
  11.7 0.2 copy.27
  12.0 0.1 eq.99
  12.1 0.1 add_reduce_fusion
  12.2 0.2 convolution_convert_fusion.2
  12.5 2.8 stack.3
  15.2 10.1 %all-to-all-start = ((bf16[16,1,8,128,128]{4,2,3,1,0:T(8,128)(2,1)}), bf16[16,1,8,128,128]{4,2,3,1,0:T(8,128)(2,1)}, u32[]{:S(2)}, u32[]{:S(2)}) async-start(bf16[16,1,8,128,128]{4,2,3,1,0:T(8,128)(2,1)} %stack.3), calls=%async_computation | async-start | bytes 8388608 | tf_op jit(solution)/shard_map/all_to_all | solution.py:11
  25.4 0.7 all-gather.7.cloned.1.call-update
  26.4 65.5 %all-gather.1 = s32[16,1,16]{2,1,0:T(1,128)S(1)} all-gather(s32[1,1,16]{2,1,0:T(1,128)S(1)} %reshape.140), channel_id=1, replica_groups=mesh['tok'=16,'hid'=32] {'tok'}, dimensions={0}, use_global_device_ids=true | all-gather | bytes 1088 | tf_op jit(solution)/shard_map/all_gather | solution.py:74
  91.9 0.2 reduce_window_sum.26
  92.1 19.4 %all-gather.2 = s32[16,1,16]{2,1,0:T(1,128)S(1)} all-gather(s32[1,1,16]{2,1,0:T(1,128)S(1)} %reshape.142), channel_id=1, replica_groups=mesh['tok'=16,'hid'=32] {'tok'}, dimensions={0}, use_global_device_ids=true | all-gather | bytes 1088 | tf_op jit(solution)/shard_map/all_gather | solution.py:78
  111.5 0.2 reduce_window_sum.27
  111.7 4.2 %convolution_convert_fusion = bf16[16,16,128,128]{3,1,2,0:T(8,128)(2,1)S(1)} fusion(bf16[16,1,8,128,128]{4,2,3,1,0:T(8,128)(2,1)} %all-to-all-done, s32[16,16]{1,0:T(8,128)S(1)} %broadcast_add_fusion, pred[16,16]{1,0:T(8,128)(4,1)S(1)} %broadcast_compare_fusion), kind=kOutput, calls=%fused_computation.6 | convolution fusion | flops 71307264 | bytes 12584192 | tf_op jit(solution)/shard_map/kbs,ksij->kbij/dot_general | solution.py:41
  115.9 5.8 %copy.28 = bf16[16,4,4,128,128]{4,2,3,1,0:T(4,128)(2,1)} copy(bf16[16,4,4,128,128]{4,2,1,3,0:T(4,128)(2,1)S(1)} %bitcast.69) | data formatting | bytes 16777216 | tf_op jit(solution)/shard_map/reshape | solution.py:44
  121.7 2.0 all-gather.11.cloned.1.call-done
  123.7 4.2 %convolution_convert_fusion.1 = bf16[16,16,128,128]{3,1,2,0:T(8,128)(2,1)S(1)} fusion(s32[16,16]{1,0:T(8,128)S(1)} %broadcast_add_fusion.1, pred[16,16]{1,0:T(8,128)(4,1)S(1)} %broadcast_compare_fusion.1, bf16[128,128,128]{2,0,1:T(8,128)(2,1)} %all-gather.11.cloned.1.call-done), kind=kOutput, calls=%fused_computation.7 | convolution fusion | flops 71307264 | bytes 12584192 | tf_op jit(solution)/shard_map/kbs,ksij->kbij/dot_general | solution.py:41
  128.0 5.9 %copy.25 = bf16[16,4,4,128,128]{4,2,3,1,0:T(4,128)(2,1)} copy(bf16[16,4,4,128,128]{4,2,1,3,0:T(4,128)(2,1)S(1)} %bitcast.70) | data formatting | bytes 16777216 | tf_op jit(solution)/shard_map/reshape | solution.py:44
  133.9 65.8 %all-gather.7.cloned.1.call-done = bf16[128,8192]{1,0:T(8,128)(2,1)} async-done(((bf16[128,256]{1,0:T(8,128)(2,1)}), bf16[128,8192]{1,0:T(8,128)(2,1)}) %all-gather.7.cloned.1.call-update) | async-done | bytes 2097168 | tf_op jit(solution)/shard_map/all_gather | solution.py:59
  199.7 6.5 %fusion.8 = f32[128,512]{0,1:T(8,128)S(1)} fusion(bf16[128,8192]{1,0:T(8,128)(2,1)} %all-gather.7.cloned.1.call-done, bf16[1024,8,4,128]{3,2,1,0:T(4,128)(2,1)} %bitcast.72), kind=kOutput, calls=%fused_computation.12 | convolution fusion | flops 1073741824 | bytes 10747904 | tf_op jit(solution)/shard_map/dot_general | solution.py:66
  206.2 0.5 copy-done.5
  206.6 3.2 fusion.17
  210.0 56.7 %all-gather.9.cloned.1.call-done = bf16[2048,512]{0,1:T(8,128)(2,1)} async-done(((bf16[128,512]{0,1:T(8,128)(2,1)}), bf16[2048,512]{0,1:T(8,128)(2,1)}) %all-gather.9.cloned.1.call-update) | async-done | bytes 2097168 | tf_op jit(solution)/shard_map/all_gather | solution.py:83
  266.7 0.2 mul.20
  266.9 4.8 %fusion.20 = f32[2048,512]{1,0:T(8,128)} fusion(bf16[2048,512]{0,1:T(8,128)(2,1)} %all-gather.9.cloned.1.call-done, bf16[512,512]{1,0:T(8,128)(2,1)S(1)} %copy-done.1, bf16[64,8,4,128]{3,2,1,0:T(4,128)(2,1)S(1)} %bitcast.73), kind=kOutput, calls=%fused_computation.17 | convolution fusion | flops 1074003968 | bytes 7340032 | tf_op jit(solution)/shard_map/dot_general | solution.py:82
  271.7 116.7 %reduce-scatter.2.cloned.1.call-done = f32[64,512]{1,0:T(8,128)} async-done(((f32[2048,512]{1,0:T(8,128)}), f32[64,512]{1,0:T(8,128)}) %reduce-scatter.2.cloned.1.call-update) | async-done | bytes 131088 | tf_op jit(solution)/shard_map/reduce_scatter | solution.py:87
  388.4 1.5 convert_element_type.32
  (31 shorter events, 0.6 us)
Async XLA Ops:
  6.5 5.4 %copy-start.3 = (s32[4,4]{1,0:T(4,128)S(1)}, s32[4,4]{1,0:T(4,128)}, u32[]{:S(2)}) copy-start(s32[4,4]{1,0:T(4,128)} %param.12) | copy-start | bytes 196
  6.5 117.2 %all-gather.11.cloned.1.call-start = ((), (), s32[]{:S(2)}) async-start(), calls=%async_computation.5 | async-start | bytes 4456448 | tf_op jit(solution)/shard_map/all_gather | solution.py:73
  15.2 10.9 %copy-start.2 = (s32[4,4]{1,0:T(4,128)S(1)}, s32[4,4]{1,0:T(4,128)}, u32[]{:S(2)}) copy-start(s32[4,4]{1,0:T(4,128)} %param.11) | copy-start | bytes 196
  15.2 96.4 %all-to-all-start = ((bf16[16,1,8,128,128]{4,2,3,1,0:T(8,128)(2,1)}), bf16[16,1,8,128,128]{4,2,3,1,0:T(8,128)(2,1)}, u32[]{:S(2)}, u32[]{:S(2)}) async-start(bf16[16,1,8,128,128]{4,2,3,1,0:T(8,128)(2,1)} %stack.3), calls=%async_computation | async-start | bytes 8388608 | tf_op jit(solution)/shard_map/all_to_all | solution.py:11
  25.4 174.3 %all-gather.7.cloned.1.call-start = ((), (), s32[]{:S(2)}) async-start(), calls=%async_computation.2 | async-start | bytes 2162688 | tf_op jit(solution)/shard_map/all_gather | solution.py:59
  26.1 240.5 %all-gather.9.cloned.1.call-start = ((), (), s32[]{:S(2)}) async-start(), calls=%async_computation.3 | async-start | bytes 2228224 | tf_op jit(solution)/shard_map/all_gather | solution.py:83
  199.7 6.5 %copy-start = (bf16[16,4,4,128,128]{4,2,3,1,0:T(4,128)(2,1)S(1)}, bf16[16,4,4,128,128]{4,2,3,1,0:T(4,128)(2,1)}, u32[]{:S(2)}) copy-start(bf16[16,4,4,128,128]{4,2,3,1,0:T(4,128)(2,1)} %copy.28) | copy-start | bytes 25165828
  199.7 7.0 %copy-start.5 = (bf16[128,8192]{1,0:T(8,128)(2,1)S(1)}, bf16[128,8192]{1,0:T(8,128)(2,1)}, u32[]{:S(2)}) copy-start(bf16[128,8192]{1,0:T(8,128)(2,1)} %all-gather.7.cloned.1.call-done) | copy-start | bytes 6291460
  206.6 3.3 copy-start.4
  206.6 60.2 %copy-start.1 = (bf16[512,512]{1,0:T(8,128)(2,1)S(1)}, bf16[512,512]{1,0:T(8,128)(2,1)}, u32[]{:S(2)}) copy-start(bf16[512,512]{1,0:T(8,128)(2,1)} %param.10) | copy-start | bytes 1572868
  209.9 178.5 %reduce-scatter.2.cloned.1.call-start = ((), (), s32[]{:S(2)}) async-start(), calls=%async_computation.4 | async-start | bytes 4325376 | tf_op jit(solution)/shard_map/reduce_scatter | solution.py:87
Sparse Core Ops, SparseCore 0:
  10.7 113.0 all-gather.10
  125.8 73.8 all-gather.6
  210.0 56.6 all-gather.8
  271.9 116.5 reduce-scatter.1
